TPU v7x, 32 devices: a whole 2x2x4 slice. The times are simulated.
32 devices in a mesh: tok: 8 (over z, y), grp: 4 (over x, core).
Axes of the slice: x: 2, y: 2, z: 4, core: 2. Of those that a mesh axis runs over, the one named last changes fastest.
Arguments:
- tokens: bfloat16 [4, 8192, 768], P('grp', 'tok'), may hold values from -6 to 6
- upstream: bfloat16 [4, 8192, 768], P('grp', 'tok'), may hold values from -6 to 6
- cluster_pos: int32 [4, 12, 8192], P('grp', None, 'tok'), may hold values from 0 to 8191, as said below
- project_in: bfloat16 [768, 2304], P(('tok', 'grp')), may hold values from -0.21875 to 0.21875
- query_bias: bfloat16 [768], P(('tok', 'grp')), may hold values from -3 to 3
- value_bias: bfloat16 [768], P(('tok', 'grp')), may hold values from -3 to 3
- project_out: bfloat16 [768, 768], P(('tok', 'grp')), may hold values from -1.25 to 1.25
- output_bias: bfloat16 [768], P(('tok', 'grp')), may hold values from -2 to 2
- first_gain: bfloat16 [768], P(('tok', 'grp')), may hold values from 0.5 to 1.5
- first_shift: bfloat16 [768], P(('tok', 'grp')), may hold values from -2 to 2
- expand: bfloat16 [768, 3072], P(('tok', 'grp')), may hold values from -0.21875 to 0.21875
- expand_bias: bfloat16 [3072], P(('tok', 'grp')), may hold values from -2 to 2
- contract: bfloat16 [3072, 768], P(('tok', 'grp')), may hold values from -0.109375 to 0.109375
- contract_bias: bfloat16 [768], P(('tok', 'grp')), may hold values from -2 to 2
- second_gain: bfloat16 [768], P(('tok', 'grp')), may hold values from 0.5 to 1.5
- second_shift: bfloat16 [768], P(('tok', 'grp')), may hold values from -2 to 2
Outputs:
- activations: bfloat16 [4, 8192, 768], P('grp', 'tok')
- token_grad: float32 [4, 8192, 768], P('grp', 'tok')
- project_in_grad: float32 [768, 2304], P(('tok', 'grp'))
- query_bias_grad: float32 [768], P(('tok', 'grp'))
- value_bias_grad: float32 [768], P(('tok', 'grp'))
- project_out_grad: float32 [768, 768], P(('tok', 'grp'))
- output_bias_grad: float32 [768], P(('tok', 'grp'))
- first_gain_grad: float32 [768], P(('tok', 'grp'))
- first_shift_grad: float32 [768], P(('tok', 'grp'))
- expand_grad: float32 [768, 3072], P(('tok', 'grp'))
- expand_bias_grad: float32 [3072], P(('tok', 'grp'))
- contract_grad: float32 [3072, 768], P(('tok', 'grp'))
- contract_bias_grad: float32 [768], P(('tok', 'grp'))
- second_gain_grad: float32 [768], P(('tok', 'grp'))
- second_shift_grad: float32 [768], P(('tok', 'grp'))
Inputs may be any that keep to these rules, and one draw needn't show every extreme that they name: `cluster_pos`: positions of one group and head form a permutation of the group's rows that maps each aligned block of 4096 rows onto itself. A block is either one sequence of 4096 tokens, in which every device of the block sends exactly 256 of its rows to every device of the block, itself included, or 8 sequences of 512 tokens, each permuted within itself. Each group has 2 blocks; on this slice both are of the first kind. Every cluster holds tokens of one sequence.
All inputs are finite; a program needn't handle non-finite values.
Results may differ from a plain program's by a relative error of at most 0.013.
Values may be sent and summed in bfloat16 or wider, within the bound.
A program may use at most 192 MiB of HBM per device.

v0:
```python
import functools
import jax
import jax.numpy as jnp
from jax import lax
from jax.experimental import pallas as pl
from jax.experimental.pallas import tpu as pltpu
from jax.sharding import PartitionSpec as P

CL = 128
LONG = 4096
F32 = jnp.float32
BF = jnp.bfloat16
VMEM_ALL = 64 * 1024 * 1024 - 65536

epsilon = 1e-05
root_half = 0.7071067811865476
density_norm = 0.3989422804014327

def normalize(hidden, gain, shift):
    centred = hidden - jnp.mean(hidden, axis=1, keepdims=True)
    inverse_std = lax.rsqrt(jnp.mean(centred * centred, axis=1, keepdims=True) + epsilon)
    unit = centred * inverse_std
    return (unit * gain + shift, unit, inverse_std)


def normalize_back(grad_out, gain, unit, inverse_std):
    scaled = grad_out * gain
    return inverse_std * (
        scaled
        - jnp.mean(scaled, axis=1, keepdims=True)
        - unit * jnp.mean(scaled * unit, axis=1, keepdims=True)
    )


def nt(a,b): return lax.dot_general(a,b,(((1,),(1,)),((),())),preferred_element_type=F32)
def nn(a,b): return lax.dot_general(a,b,(((1,),(0,)),((),())),preferred_element_type=F32)
def tn(a,b): return lax.dot_general(a,b,(((0,),(0,)),((),())),preferred_element_type=F32)

def fwd_kernel(span, pos, tok, w, bias, *refs):
    leave = refs[:span]
    left, right, src, ord_, oc = refs[span:]
    h=pl.program_id(0)
    n=tok.shape[0]
    ch=512
    def proj(i,_):
        r=pl.multiple_of(i*ch,ch)
        acc=nn(tok[pl.ds(r,ch),:],w[...])+bias[0]
        src[pl.ds(2*r,ch,stride=2),:]=acc[:,:128]
        src[pl.ds(2*r+1,ch,stride=2),:]=acc[:,128:]
        return 0
    lax.fori_loop(0,n//ch,proj,0)
    U=64
    def scat(i,_):
        for u in range(U):
            t=i*U+u
            ord_[pl.ds(2*pos[h*n+t],2),:]=src[pl.ds(2*t,2),:]
        return 0
    lax.fori_loop(0,n//U,scat,0)
    CB=4
    def clus(i,_):
        for u in range(CB):
            r=pl.multiple_of((i*CB+u)*CL,CL)
            l=ord_[pl.ds(2*r,CL,stride=2),:].astype(BF)
            rr=ord_[pl.ds(2*r+1,CL,stride=2),:].astype(BF)
            left[0,pl.ds(r,CL),:]=l
            right[0,pl.ds(r,CL),:]=rr
            s=nt(rr,l)
            m=jnp.max(s,axis=0,keepdims=True)
            e=jnp.exp((s-m)*0.125)
            p=(e*(1.0/jnp.sum(e,axis=0,keepdims=True))).astype(BF)
            oc[pl.ds(r,CL),:]=tn(p,rr)
        return 0
    lax.fori_loop(0,n//CL//CB,clus,0)
    def gath(i,_):
        for u in range(U):
            t=i*U+u
            src[pl.ds(t,1),:]=oc[pl.ds(pos[h*n+t],1),:]
        return 0
    lax.fori_loop(0,n//U,gath,0)
    count=n//span
    @pl.when(h==0)
    def _():
        for k in range(span):
            leave[k][:count,:64]=src[k*count:(k+1)*count,:64].astype(BF)
    @pl.when(h==1)
    def _():
        for k in range(span):
            leave[k][:count,64:]=src[k*count:(k+1)*count,64:].astype(BF)
    @pl.when(h==2)
    def _():
        for k in range(span):
            mid_row=k*count+count//2
            leave[k][count:,:64]=src[k*count:mid_row,64:].astype(BF)
            leave[k][count:,64:]=src[mid_row:(k+1)*count,64:].astype(BF)

def fwd(pos,tok,w,bias,span):
    rows=tok.shape[0]//span*3//2
    n=tok.shape[0]; H=pos.shape[0]//n
    return pl.pallas_call(functools.partial(fwd_kernel,span),grid=(H,),
      out_shape=(jax.ShapeDtypeStruct((rows,128),BF),)*span+(jax.ShapeDtypeStruct((H,n,128),BF),)*2,
      in_specs=[pl.BlockSpec(memory_space=pltpu.SMEM),
                pl.BlockSpec((n,tok.shape[1]),lambda h:(0,0)),
                pl.BlockSpec((tok.shape[1],256),lambda h:(0,h)),
                pl.BlockSpec((1,1,256),lambda h: (h, 0, 0))],
      out_specs=(pl.BlockSpec((rows,128),lambda h: (0, 0)),)*span+(pl.BlockSpec((1,n,128),lambda h: (h, 0, 0)),)*2,
      scratch_shapes=[pltpu.VMEM((2*n,128),F32),pltpu.VMEM((2*n,128),F32),pltpu.VMEM((n,128),F32)],
      compiler_params=pltpu.CompilerParams(vmem_limit_bytes=VMEM_ALL),name="att_fwd")(pos,tok,w,bias)

def bwd_kernel(span, pos, left, right, *refs):
    landed = refs[:span]
    gj, total, src, ord_, dc = refs[span:]
    h=pl.program_id(0)
    n=left.shape[1]
    U=64
    count=n//span
    @pl.when(h<2)
    def _():
        for k in range(span):
            src[k*count:(k+1)*count,:]=landed[k][:count,:].astype(F32)
    @pl.when(h==2)
    def _():
        for k in range(span):
            x=landed[k][count:,:].astype(F32)
            mid_row=k*count+count//2
            src[k*count:mid_row,:]=jnp.concatenate([x[:,64:],x[:,:64]],axis=1)
            src[mid_row:(k+1)*count,:]=x
    def scat(i,_):
        for u in range(U):
            t=i*U+u
            ord_[pl.ds(pos[h*n+t],1),:]=src[pl.ds(t,1),:]
        return 0
    lax.fori_loop(0,n//U,scat,0)
    lane=lax.broadcasted_iota(jnp.int32,(CL,128),1)
    mask=(lane<64)==(h==0)
    CB=4
    def clus(i,_):
        for u in range(CB):
            r=pl.multiple_of((i*CB+u)*CL,CL)
            l=left[0,pl.ds(r,CL),:]
            rr=right[0,pl.ds(r,CL),:]
            d=jnp.where(mask,ord_[pl.ds(r,CL),:],0.0).astype(BF)
            s=nt(rr,l)
            m=jnp.max(s,axis=0,keepdims=True)
            e=jnp.exp((s-m)*0.125)
            p=e*(1.0/jnp.sum(e,axis=0,keepdims=True))
            dp=nt(rr,d)
            rd=jnp.sum(dp*p,axis=0,keepdims=True)
            ds=(p*(dp-rd)).astype(BF)
            dl=tn(ds,rr)*0.125
            dr=nn(ds,l)*0.125+nn(p.astype(BF),d)
            dc[pl.ds(2*r,CL,stride=2),:]=dl
            dc[pl.ds(2*r+1,CL,stride=2),:]=dr
        return 0
    lax.fori_loop(0,n//CL//CB,clus,0)
    def gath(i,_):
        for u in range(U):
            t=i*U+u
            src[pl.ds(2*t,2),:]=dc[pl.ds(2*pos[h*n+t],2),:]
        return 0
    lax.fori_loop(0,n//U,gath,0)
    ch=512
    def out(i,sums):
        r=pl.multiple_of(i*ch,ch)
        one=src[pl.ds(2*r,ch,stride=2),:].astype(BF)
        two=src[pl.ds(2*r+1,ch,stride=2),:].astype(BF)
        gj[pl.ds(r,ch),:128]=one
        gj[pl.ds(r,ch),128:]=two
        fold=lambda x: jnp.sum(x.astype(F32).reshape(ch//8,8,128),axis=0)
        return (sums[0]+fold(one),sums[1]+fold(two))
    zero=jnp.zeros((8,128),F32)
    one,two=lax.fori_loop(0,n//ch,out,(zero,zero))
    total[:,:128]=one
    total[:,128:]=two

def bwd(pos,left,right,landed):
    H,n=left.shape[:2]
    span=len(landed)
    rows=landed[0].shape[0]
    blk=lambda: pl.BlockSpec((1,n,128),lambda h: (h, 0, 0))
    return pl.pallas_call(functools.partial(bwd_kernel,span),grid=(H,),
      out_shape=(jax.ShapeDtypeStruct((n,H*256),BF),jax.ShapeDtypeStruct((8,H*256),F32)),
      in_specs=[pl.BlockSpec(memory_space=pltpu.SMEM),blk(),blk()]+[pl.BlockSpec((rows,128),lambda h: (0, 0))]*span,
      out_specs=(pl.BlockSpec((n,256),lambda h: (0, h)),pl.BlockSpec((8,256),lambda h: (0, h))),
      scratch_shapes=[pltpu.VMEM((2*n,128),F32),pltpu.VMEM((n,128),F32),pltpu.VMEM((2*n,128),F32)],
      compiler_params=pltpu.CompilerParams(vmem_limit_bytes=VMEM_ALL),name="att_bwd")(pos,left,right,*landed)

def mid_kernel(span, *refs):
    came = refs[:span]
    at, tok, up, wo, we, wc, vec, ebias = refs[span:span + 8]
    result, gfirst = refs[span + 8:span + 10]
    leave = refs[span + 10:2 * span + 10]
    merged_o, gbranch_o, nlow_o, gmid_o, lifted_o, ginner_o, sums, esum = refs[2 * span + 10:2 * span + 18]
    wop, slope = refs[2 * span + 18:]
    i = pl.program_id(0)
    rows, width = tok.shape
    half = rows * pl.num_programs(0) // 2
    strips = we.shape[0]
    own = width // span
    pair = 128
    single = own - pair

    @pl.when(i == 0)
    def _():
        for k in range(span):
            p = pl.multiple_of((at[0] ^ k) * own, 64)
            wop[k * pair:(k + 1) * pair, :] = wo[pl.ds(p, pair), :]
            wop[span * pair + k * single:span * pair + (k + 1) * single, :] = wo[pl.ds(p + pair, single), :]
        sums[...] = jnp.zeros_like(sums)
        esum[...] = jnp.zeros_like(esum)

    def total(at_row, value):
        sums[at_row:at_row + 1, :] += jnp.sum(value, axis=0, keepdims=True)

    low = i * rows < half
    start = pl.multiple_of(2 * half + lax.rem(i * rows, half), rows)
    pairs = [c[pl.ds(pl.multiple_of(i * rows, rows), rows), :] for c in came]
    both = [c[pl.ds(start, rows), :] for c in came]
    singles = [jnp.where(low, x[:, :single], x[:, single:]) for x in both]
    merged = jnp.concatenate(pairs + singles, axis=1)
    merged_o[...] = merged
    hidden = tok[...].astype(F32) + nn(merged, wop[...]) + vec[0:1, :]
    normed_one, unit_one, inverse_one = normalize(hidden, vec[1:2, :], vec[2:3, :])
    normed_low = normed_one.astype(BF)
    nlow_o[...] = normed_low
    second = normed_one + vec[3:4, :]
    for k in range(strips):
        cols = slice(k * width, (k + 1) * width)
        inner = nn(normed_low, we[k]) + ebias[k:k + 1, :]
        cdf = 0.5 * (1.0 + lax.erf(inner * root_half))
        lifted = (inner * cdf).astype(BF)
        slope[:, cols] = cdf + inner * jnp.exp(-0.5 * inner * inner) * density_norm
        lifted_o[:, cols] = lifted
        second += nn(lifted, wc[cols, :])
    out, unit_two, inverse_two = normalize(second, vec[4:5, :], vec[5:6, :])
    result[...] = out.astype(BF)
    cotangent = up[...].astype(F32)
    total(0, cotangent * unit_two)
    total(1, cotangent)
    grad_second = normalize_back(cotangent, vec[4:5, :], unit_two, inverse_two)
    grad_mid = grad_second.astype(BF)
    gmid_o[...] = grad_mid
    total(2, grad_mid.astype(F32))
    grad_normed = grad_second
    for k in range(strips):
        cols = slice(k * width, (k + 1) * width)
        grad_inner = (nt(grad_mid, wc[cols, :]) * slope[:, cols]).astype(BF)
        ginner_o[:, cols] = grad_inner
        esum[k:k + 1, :] += jnp.sum(grad_inner.astype(F32), axis=0, keepdims=True)
        grad_normed += nt(grad_inner, we[k])
    total(3, grad_normed * unit_one)
    total(4, grad_normed)
    grad_first = normalize_back(grad_normed, vec[1:2, :], unit_one, inverse_one)
    gfirst[...] = grad_first
    grad_branch = grad_first.astype(BF)
    gbranch_o[...] = grad_branch
    total(5, grad_branch.astype(F32))
    grad_merged = nt(grad_branch, wop[...]).astype(BF)
    for k in range(span):
        leave[k][pl.ds(pl.multiple_of(i * rows, rows), rows), :] = grad_merged[:, k * pair:(k + 1) * pair]
        one = grad_merged[:, span * pair + k * single:span * pair + (k + 1) * single]

        @pl.when(low)
        def _():
            leave[k][pl.ds(start, rows), :single] = one

        @pl.when(jnp.logical_not(low))
        def _():
            leave[k][pl.ds(start, rows), single:] = one


def mid(came, at, tok, up, wo, we, wc, vec, ebias, rows=256):
    span = len(came)
    count, width = tok.shape
    strips = we.shape[0]
    S = jax.ShapeDtypeStruct
    vm = pl.BlockSpec(memory_space=pltpu.VMEM)
    tile = lambda w: pl.BlockSpec((rows, w), lambda i: (i, 0))
    fixed = lambda shape: pl.BlockSpec(shape, lambda i: (0, 0))
    deep = strips * width
    outs = (
        [(S((count, width), BF), tile(width)), (S((count, width), F32), tile(width))]
        + [(S(came[0].shape, BF), fixed(came[0].shape))] * span
        + [(S((count, width), BF), tile(width))] * 4
        + [(S((count, deep), BF), tile(deep))] * 2
        + [(S((8, width), F32), fixed((8, width))), (S((strips, width), F32), fixed((strips, width)))]
    )
    return pl.pallas_call(
        functools.partial(mid_kernel, span),
        grid=(count // rows,),
        out_shape=[o for o, _ in outs],
        in_specs=[vm] * span + [pl.BlockSpec(memory_space=pltpu.SMEM), tile(width), tile(width)] + [vm] * 5,
        out_specs=[b for _, b in outs],
        scratch_shapes=[pltpu.VMEM((width, width), BF), pltpu.VMEM((rows, deep), F32)],
        compiler_params=pltpu.CompilerParams(vmem_limit_bytes=VMEM_ALL),
        name="mid",
    )(*came, at, tok, up, wo, we, wc, vec, ebias)

MESH = pl.DeviceIdType.MESH


def bits_of(size):
    return size.bit_length() - 1


def steps_of(nt, ng):
    return [("tok", b) for b in reversed(range(bits_of(nt)))] + [
        ("grp", b) for b in reversed(range(bits_of(ng)))
    ]


def greet(peers):
    barrier = pltpu.get_barrier_semaphore()
    for peer in peers:
        pl.semaphore_signal(barrier, inc=1, device_id=peer, device_id_type=MESH)
    pl.semaphore_wait(barrier, len(peers))


def collect_kernel(nt, ng, parts, *refs):
    tok_in, pos_in, pin_in = refs[:3]
    nf = (len(refs) - 13) // 2
    full_in = refs[3:3 + nf]
    tok_out, pos_out, pin_out = refs[3 + nf:6 + nf]
    full_out = refs[6 + nf:6 + 2 * nf]
    lsem, tsend, trecv, psend, precv, wsend, wrecv = refs[6 + 2 * nf:]
    t = lax.axis_index("tok")
    g = lax.axis_index("grp")
    steps = steps_of(nt, ng)
    nb = len(steps)
    me = t * ng + g
    digits = [(me // (1 << (nb - 1 - j))) % 2 for j in range(nb)]

    def held_at(s):
        return (slice(None),) * s + tuple(digits[s:])

    def peer(axis, mask):
        return {"tok": t ^ mask, "grp": g} if axis == "tok" else {"tok": t, "grp": g ^ mask}

    count = tok_in.shape[0]
    own = [pltpu.make_async_copy(tok_in, tok_out.at[0], lsem.at[0]),
           pltpu.make_async_copy(pos_in.at[t % 4], pos_out.at[0], lsem.at[1])]
    for i, (a, b) in enumerate(zip(full_in, full_out)):
        own.append(pltpu.make_async_copy(a, b.at[held_at(0)], lsem.at[2 + i]))
    greet([peer(axis, 1 << b) for axis, b in steps] + [peer("tok", 3)])
    for copy in own:
        copy.start()

    flights = {}

    def send(name, src, dst, sems, to):
        copy = pltpu.make_async_remote_copy(
            src_ref=src, dst_ref=dst, send_sem=sems[0], recv_sem=sems[1],
            device_id=to, device_id_type=MESH)
        copy.start()
        flights[name] = copy

    arrived = set()

    def wait(name):
        if name not in arrived:
            arrived.add(name)
            flights[name].wait_recv()

    chunk = count // parts

    def rows(c):
        return pl.ds(c * chunk, chunk)

    def token(c, mask):
        i = (mask - 1) * parts + c
        send(("t", mask, c), tok_in.at[rows(c)], tok_out.at[mask, rows(c)],
             (tsend.at[i], trecv.at[i]), peer("tok", mask))

    def relay(c):
        i = 2 * parts + c
        mask = 2 if c >= parts // 2 else 1
        wait(("t", 3 - mask, c))
        send(("r", c), tok_out.at[3 - mask, rows(c)], tok_out.at[3, rows(c)],
             (tsend.at[i], trecv.at[i]), peer("tok", mask))

    def position(mask):
        i = mask - 1
        send(("p", mask), pos_in.at[(t ^ mask) % 4], pos_out.at[mask],
             (psend.at[i], precv.at[i]), peer("tok", mask))

    def full(w, s):
        axis, b = steps[s]
        i = w * nb + s
        to = peer(axis, 1 << b)
        out = full_out[w]
        if s == 0:
            src, dst = full_in[w], out.at[held_at(0)]
        else:
            wait(("w", w, s - 1))
            if s == 1:
                own[2 + w].wait()
            src = out.at[held_at(s)]
            dst = src
        send(("w", w, s), src, dst, (wsend.at[i], wrecv.at[i]), to)

    def slices(s):
        axis, b = steps[s]
        i = nf * nb + s
        to = peer(axis, 1 << b)
        tb = bits_of(nt)
        if s > 0:
            wait(("w", nf, s - 1))
        high = tb - 2
        theirs = (t ^ (1 << b)) if axis == "tok" else t
        if s < high:
            place = (slice(None), slice(None))
        elif s == high:
            place = ((theirs // 2) % 2, slice(None))
        else:
            place = ((theirs // 2) % 2, theirs % 2)
        src = pin_out.at[place + held_at(s)]
        send(("w", nf, s), src, src, (wsend.at[i], wrecv.at[i]), to)

    pin_own = pltpu.make_async_copy(pin_in, pin_out.at[(slice(None), slice(None)) + held_at(0)], lsem.at[2 + nf])
    pin_own.start()
    order = list(range(nf))
    half = parts // 2
    for c in range(half):
        token(c, 1)
    for w in order:
        full(w, 0)
    pin_own.wait()
    slices(0)
    for mask in (1, 2, 3):
        position(mask)
    token(0, 2)
    done_y, done_z = half, 1
    for s in range(1, nb):
        for w in order:
            full(w, s)
            if w >= 0:
                if done_z < parts:
                    token(done_z, 2)
                    done_z += 1
                if done_y < parts and s >= 2:
                    token(done_y, 1)
                    done_y += 1
        slices(s)
        if s == nb - 2:
            for c in range(done_z, parts):
                token(c, 2)
            for c in range(done_y, parts):
                token(c, 1)
            for c in range(parts):
                relay(c)
    own[0].wait()
    own[1].wait()
    if nb == 1:
        for w in range(nf):
            own[2 + w].wait()
    for name in flights:
        wait(name)
    for copy in flights.values():
        copy.wait_send()


def collect(nt, ng, tokens, pos, pin, fulls, parts=4):
    n = nt * ng
    nb = bits_of(nt) + bits_of(ng)
    hbm = pl.BlockSpec(memory_space=pl.ANY)
    vm = pl.BlockSpec(memory_space=pltpu.VMEM)
    S = jax.ShapeDtypeStruct
    block, at, own, *wide = pl.pallas_call(
        functools.partial(collect_kernel, nt, ng, parts),
        out_shape=[S((4,) + tokens.shape, tokens.dtype), S((4,) + pos.shape[1:], pos.dtype),
                   S((2, 2) + (2,) * nb + pin.shape[1:], pin.dtype)] + [S((2,) * nb + f.shape, f.dtype) for f in fulls],
        in_specs=[vm] * (3 + len(fulls)),
        out_specs=[hbm] * (3 + len(fulls)),
        scratch_shapes=[
            pltpu.SemaphoreType.DMA((3 + len(fulls),)),
            pltpu.SemaphoreType.DMA((3 * parts,)), pltpu.SemaphoreType.DMA((3 * parts,)),
            pltpu.SemaphoreType.DMA((3,)), pltpu.SemaphoreType.DMA((3,)),
            pltpu.SemaphoreType.DMA(((len(fulls) + 1) * nb,)), pltpu.SemaphoreType.DMA(((len(fulls) + 1) * nb,)),
        ],
        compiler_params=pltpu.CompilerParams(collective_id=0, has_side_effects=True),
        name="collect",
    )(tokens, pos, pin.reshape((2, 2) + pin.shape[1:]), *fulls)
    return [block, at, own.reshape((4, n) + pin.shape[1:])] + [
        w.reshape((n,) + f.shape) for w, f in zip(wide, fulls)]


def reduce_kernel(nt, ng, *refs):
    pin_in, small_in, pin_out, small_out = refs[:4]
    nb = bits_of(nt) + bits_of(ng)
    tb = bits_of(nt)
    pin_a, small_a, quad = refs[4:7]
    landing = refs[7:7 + 2 * nb]
    ssem, rsem = refs[7 + 2 * nb:]
    t = lax.axis_index("tok")
    g = lax.axis_index("grp")
    steps = steps_of(nt, ng)
    me = t * ng + g
    digits = [(me // (1 << (nb - 1 - j))) % 2 for j in range(nb)]

    def peer(s):
        axis, b = steps[s]
        mask = 1 << b
        return {"tok": t ^ mask, "grp": g} if axis == "tok" else {"tok": t, "grp": g ^ mask}

    greet([peer(s) for s in range(nb)])
    p1, p0 = (t // 2) % 2, t % 2
    flying = []

    def launch(i, src, dst, s):
        copy = pltpu.make_async_remote_copy(
            src_ref=src, dst_ref=dst, send_sem=ssem.at[i], recv_sem=rsem.at[i],
            device_id=peer(s), device_id_type=MESH)
        copy.start()
        flying.append(copy)
        return copy

    def away(s):
        return (slice(None),) * s + (1 - digits[s],) + tuple(digits[s + 1:])

    def kept(s):
        return (slice(None),) * s + tuple(digits[s:])

    def add(ref, at, other, dst, to):
        value = ref[at].astype(F32) + other[...].astype(F32)
        dst[to] = value.astype(dst.dtype)

    for s in reversed(range(nb)):
        first = s == nb - 1
        outer = s >= tb
        sources = [pin_in if first else pin_a, small_in if first else small_a]
        copies = []
        for w in range(2):
            land = landing[w * nb + s]
            i = w * nb + s
            if w == 0 and not outer:
                place = {tb - 1: (p1, p0), tb - 2: (p1, slice(None))}.get(s, (slice(None), slice(None)))
                cut = (slice(None),) * s + (1 - digits[s],) + tuple(digits[s + 1:tb])
                src = quad.at[place + cut]
                copies.append(launch(i, src, src if s >= tb - 2 else land, s))
            else:
                copies.append(launch(i, sources[w].at[away(s)], land, s))
        for w in range(2):
            copies[w].wait_recv()
            land = landing[w * nb + s]
            if w == 0 and not outer:
                if s < tb - 2:
                    at = (slice(None), slice(None)) + (slice(None),) * s + tuple(digits[s:tb])
                    add(quad, at, land, quad, at)
            elif w == 0 and s == tb:
                add(sources[0], kept(s), land, quad, (p1, p0))
            else:
                dst = (pin_a, small_a)[w]
                add(sources[w], kept(s), land, dst, kept(s))
    for copy in flying:
        copy.wait_send()
    pin_out[...] = quad[(slice(None), slice(None)) + tuple(digits[:tb])]
    small_out[...] = small_a[tuple(digits)]


def reduce_small(nt, ng, pin, small):
    nb = bits_of(nt) + bits_of(ng)
    tb = bits_of(nt)
    two = (2,) * nb
    r, c = pin.shape[1:]
    rs = small.shape[1:]
    S = jax.ShapeDtypeStruct
    vm = pl.BlockSpec(memory_space=pltpu.VMEM)
    landing = []
    for w, (shape, dt) in enumerate((((r, c), BF), (rs, F32))):
        for s in range(nb):
            lead = (2,) * s
            if w == 0 and s < tb:
                lead = ((2, 2) + lead) if s < tb - 2 else (1,)
                landing.append(pltpu.VMEM(lead + (shape if s < tb - 2 else (8, 128)), dt))
            else:
                landing.append(pltpu.VMEM(lead + shape, dt))
    return pl.pallas_call(
        functools.partial(reduce_kernel, nt, ng),
        out_shape=[S((2, 2, r, c), BF), S(rs, F32)],
        in_specs=[vm] * 2,
        out_specs=[vm] * 2,
        scratch_shapes=[
            pltpu.VMEM(two + (r, c), BF), pltpu.VMEM(two + rs, F32),
            pltpu.VMEM((2, 2) + (2,) * tb + (r, c), BF),
        ] + landing + [pltpu.SemaphoreType.DMA((2 * nb,)), pltpu.SemaphoreType.DMA((2 * nb,))],
        compiler_params=pltpu.CompilerParams(collective_id=1, has_side_effects=True, vmem_limit_bytes=VMEM_ALL),
        name="reduce_small",
    )(pin.reshape(two + (r, c)), small.reshape(two + rs))


def flip(block, mask):
    count = lax.axis_size("tok")
    return lax.ppermute(block, "tok", [(i, i ^ mask) for i in range(count)])


def gather_all(item):
    return lax.all_gather(item, ("tok", "grp"), axis=0, tiled=True)


def scatter_sum(item):
    return lax.psum_scatter(item, ("tok", "grp"), scatter_dimension=0, tiled=True)


def shards(
    tokens,
    upstream,
    cluster_pos,
    project_in,
    query_bias,
    value_bias,
    project_out,
    output_bias,
    first_gain,
    first_shift,
    expand,
    expand_bias,
    contract,
    contract_bias,
    second_gain,
    second_shift,
):
    inputs = tokens[0]
    count, width = inputs.shape
    positions = cluster_pos[0] % LONG
    heads = positions.shape[0]
    head_dim = width // heads
    span = LONG // count
    mine = heads // span
    offset = lax.axis_index("tok") % span
    total = span * count

    nt = lax.axis_size("tok")
    ng = lax.axis_size("grp")
    devices = nt * ng
    few = query_bias.shape[0]
    strips = expand.shape[1] // width

    pieces = project_in.reshape(few, 3, span, mine, head_dim)
    hollow = jnp.zeros((few, head_dim), BF)
    arranged = []
    for place in range(span):
        columns = []
        for h in range(mine):
            query, key, value = (pieces[:, i, place, h] for i in range(3))
            columns += [hollow, query, value, key] if h == 0 else [query, hollow, key, value]
        arranged.append(jnp.concatenate(columns, axis=1))
    packed = jnp.concatenate(
        [
            query_bias, value_bias, output_bias, first_gain, first_shift,
            contract_bias, second_gain, second_shift, expand_bias,
        ]
    ).astype(F32)
    packed = jnp.pad(packed, (0, 1024 - packed.shape[0])).reshape(8, 128)
    block, own_at, arranged, packed = collect(
        nt, ng, inputs, positions.reshape(span, mine, count), jnp.stack(arranged), [packed]
    )
    wide = jnp.concatenate(
        [project_out, expand.reshape(few, strips, width).transpose(1, 0, 2).reshape(-1, width), contract],
        axis=0,
    )
    wide, packed = lax.optimization_barrier((wide, packed))
    wide = gather_all(wide[None])
    project_out = wide[:, :few]
    expand = wide[:, few : (1 + strips) * few].reshape(devices, strips, few, width)
    expand = expand.transpose(1, 0, 2, 3).reshape(strips, width, width)
    contract = wide[:, (1 + strips) * few :].reshape(strips * width, width)
    block = block.reshape(total, width)
    own_at = own_at.transpose(1, 0, 2).reshape(-1)
    arranged = lax.dynamic_index_in_dim(arranged, offset, 0, False).reshape(width, -1)
    packed = packed.reshape(devices, -1)
    vectors = packed[:, : 8 * few].reshape(devices, 8, few).transpose(1, 0, 2).reshape(8, width)
    expand_bias = packed[:, 8 * few : (8 + strips) * few].reshape(strips, width)
    query_bias, value_bias = vectors[0], vectors[1]
    vectors = jnp.concatenate([vectors[2:], vectors[:2]], axis=0)

    own_query = lax.dynamic_slice_in_dim(query_bias.reshape(heads, head_dim), offset * mine, mine)
    own_value = lax.dynamic_slice_in_dim(value_bias.reshape(heads, head_dim), offset * mine, mine)
    blank = jnp.zeros((head_dim,), F32)
    rows = []
    for h in range(mine):
        parts = [blank, own_query[h], own_value[h], blank] if h == 0 else [own_query[h], blank, blank, own_value[h]]
        rows.append(jnp.concatenate(parts))
    bias_rows = jnp.stack(rows)[:, None]

    *leaving, left, right = fwd(own_at, block, arranged, bias_rows, span)
    came = [leaving[0]] + [flip(leaving[k], k) for k in range(1, span)]
    project_out = project_out.reshape(width, width)
    result, grad_first, *rest = mid(
        came, offset[None].astype(jnp.int32), inputs, upstream[0], project_out, expand, contract,
        vectors, expand_bias,
    )
    sending = rest[:span]
    merged, grad_branch, normed_low, grad_mid, lifted, grad_inner, row_sums, expand_sums = rest[span:]
    landed = [sending[0]] + [flip(sending[k], k) for k in range(1, span)]

    def turn(item):
        item = item.reshape(2, 2, mine * head_dim, width)
        item = jnp.where(offset % 2 == 1, item[:, ::-1], item)
        return jnp.where(offset // 2 == 1, item[::-1], item).reshape(width, width)

    contract_grad = jnp.einsum("rf,rd->fd", lifted, grad_mid, preferred_element_type=F32)
    expand_grad = jnp.einsum("rd,rf->df", normed_low, grad_inner, preferred_element_type=F32)
    turned_grad = jnp.einsum("rd,re->de", merged, grad_branch, preferred_element_type=F32).astype(BF)
    split = span * 2 * head_dim
    project_out_grad = turn(
        jnp.concatenate(
            [
                turned_grad[:split].reshape(span, 2 * head_dim, width),
                turned_grad[split:].reshape(span, head_dim, width),
            ],
            axis=1,
        )
    )
    expand_grad = expand_grad.astype(BF)
    contract_grad = contract_grad.astype(BF)
    wide_grad = jnp.concatenate(
        [project_out_grad.reshape(devices, few, width)]
        + [expand_grad[:, i * width : (i + 1) * width].reshape(devices, few, width) for i in range(strips)]
        + [contract_grad.reshape(devices, strips * few, width)],
        axis=1,
    )
    landed, wide_grad = lax.optimization_barrier((landed, wide_grad))
    wide_grad = scatter_sum(wide_grad)[0].astype(F32)
    project_out_grad = wide_grad[:few]
    expand_grad = wide_grad[few : (1 + strips) * few].reshape(strips, few, width).transpose(1, 0, 2).reshape(few, -1)
    contract_grad = wide_grad[(1 + strips) * few :]
    grad_rows, grad_sums = bwd(own_at, left, right, landed)
    partial = [
        jnp.einsum(
            "re,de->rd", grad_rows[k * count : (k + 1) * count], arranged, preferred_element_type=F32
        )
        for k in range(span)
    ]
    returned = [flip(partial[k].astype(BF), k) for k in range(1, span)]
    arranged_grad = jnp.einsum("rd,re->de", block, grad_rows, preferred_element_type=F32).astype(BF)
    sums = jnp.sum(grad_sums, axis=0).reshape(mine, 4, head_dim)
    query_at = [1] + [0] * (mine - 1)
    key_at = [3] + [2] * (mine - 1)
    value_at = [2] + [3] * (mine - 1)

    def spread(take, at):
        return jnp.stack([take(h, at[h]) for h in range(mine)], axis=-2)

    own_sums = jnp.stack([spread(lambda h, s: sums[h, s], at) for at in (query_at, value_at)])
    bias_grads = lax.dynamic_update_slice_in_dim(
        jnp.zeros((2, heads, head_dim), F32), own_sums, offset * mine, axis=1
    ).reshape(2, width)
    token_grad = grad_first + partial[0]
    for item in returned:
        token_grad = token_grad + item.astype(F32)
    ordered = jnp.concatenate([bias_grads, row_sums[5:6], row_sums[3:5], row_sums[2:3], row_sums[:2]], axis=0)
    small = jnp.concatenate(
        [
            ordered.reshape(8, devices, few).transpose(1, 0, 2).reshape(devices, 8 * few),
            expand_sums.reshape(devices, strips * few),
        ],
        axis=1,
    )
    small = jnp.pad(small, ((0, 0), (0, 1024 - small.shape[1]))).reshape(devices, 8, 128)
    project_in_grad, small = reduce_small(nt, ng, arranged_grad.reshape(devices, few, -1), small)
    project_in_grad = project_in_grad.astype(F32).reshape(span, few, mine, 4, head_dim)
    project_in_grad = jnp.concatenate(
        [
            project_in_grad[place, :, h, at[h]]
            for at in (query_at, key_at, value_at)
            for place in range(span)
            for h in range(mine)
        ],
        axis=1,
    )
    small = small.reshape(-1)
    each = [small[i * few : (i + 1) * few] for i in range(8)] + [small[8 * few : (8 + strips) * few]]
    return (
        result[None],
        token_grad[None],
        project_in_grad,
        each[0],
        each[1],
        project_out_grad,
        each[2],
        each[3],
        each[4],
        expand_grad,
        each[8],
        contract_grad,
        each[5],
        each[6],
        each[7],
    )


def solution(mesh):
    placed = (
        P("grp", "tok", None),
        P("grp", "tok", None),
        P("grp", None, "tok"),
        P(("tok", "grp"), None),
        P(("tok", "grp")),
        P(("tok", "grp")),
        P(("tok", "grp"), None),
        P(("tok", "grp")),
        P(("tok", "grp")),
        P(("tok", "grp")),
        P(("tok", "grp"), None),
        P(("tok", "grp")),
        P(("tok", "grp"), None),
        P(("tok", "grp")),
        P(("tok", "grp")),
        P(("tok", "grp")),
    )
    return jax.shard_map(
        shards,
        mesh=mesh,
        in_specs=placed,
        out_specs=(
            P("grp", "tok", None),
            P("grp", "tok", None),
            P(("tok", "grp"), None),
            P(("tok", "grp")),
            P(("tok", "grp")),
            P(("tok", "grp"), None),
            P(("tok", "grp")),
            P(("tok", "grp")),
            P(("tok", "grp")),
            P(("tok", "grp"), None),
            P(("tok", "grp")),
            P(("tok", "grp"), None),
            P(("tok", "grp")),
            P(("tok", "grp")),
            P(("tok", "grp")),
        ),
        check_vma=False,
    )
```

profile of v0, /device:TPU:0, one launch (start us, length us, event | category | flops | bytes accessed | tf_op | source)
XLA Modules:
  0.0 460.6 jit_solution(15170052699488583713)
XLA Ops:
  13.6 67.1 %collect.1 = (bf16[4,1024,768]{2,1,0:T(8,128)(2,1)}, s32[4,3,1024]{2,1,0:T(4,128)}, bf16[2,2,2,2,2,2,2,24,768]{8,7,6,5,4,3,2,1,0:T(8,128)(2,1)}, f32[2,2,2,2,2,8,128]{6,5,4,3,2,1,0:T(8,128)}) custom-call(bf16[1024,768]{1,0:T(8,128)(2,1)} %bitcast.223, s32[4,3,1024]{2,1,0:T(4,128)} %add_select_fusion.refs_1_, bf16[2,2,24,768]{3,2,1,0:T(8,128)(2,1)} %bitcast.245, ...), custom_call_target="tpu_custom_call" | custom-call | tf_op jit(solution)/shard_map/collect/pallas_call | solution.py:467
  85.7 2.4 constant_dynamic-slice_fusion.2
  88.1 74.3 %att_fwd.1 = (bf16[1536,128]{1,0:T(8,128)(2,1)}, bf16[1536,128]{1,0:T(8,128)(2,1)}, bf16[1536,128]{1,0:T(8,128)(2,1)}, bf16[1536,128]{1,0:T(8,128)(2,1)}, bf16[3...) custom-call(s32[12288]{0:T(1024)} %bitcast.249, bf16[4096,768]{1,0:T(8,128)(2,1)} %bitcast.219, ...), custom_call_target="tpu_custom_call" | custom-call | tf_op jit(solution)/shard_map/att_fwd/pallas_call | solution.py:99
  170.1 2.4 slice.534
  172.5 6.5 %fusion.9 = (bf16[32,96,768]{2,1,0:T(8,128)(2,1)}, bf16[32,96,768]{2,1,0:T(8,128)(2,1)S(1)}) fusion(bf16[32,216,768]{2,1,0:T(8,128)(2,1)} %bitcast.218), kind=kLoop, calls=%fused_computation.106 | loop fusion | bytes 18874368 | tf_op jit(solution)/shard_map/slice | solution.py:665
  179.0 2.6 copy.2015
  183.1 39.9 %mid.1 = (bf16[1024,768]{1,0:T(8,128)(2,1)}, f32[1024,768]{1,0:T(8,128)}, bf16[1536,128]{1,0:T(8,128)(2,1)}, bf16[1536,128]{1,0:T(8,128)(2,1)}, bf16[1536,128]{1...) custom-call(bf16[1536,128]{1,0:T(8,128)(2,1)} %get-tuple-element.55., ...), custom_call_target="tpu_custom_call" | custom-call | tf_op jit(solution)/shard_map/mid/pallas_call | solution.py:287
  223.0 3.5 convolution_convert_fusion.6
  227.9 5.4 %convolution_convert_fusion.1 = bf16[768,3072]{1,0:T(8,128)(2,1)S(1)} fusion(bf16[1024,768]{1,0:T(8,128)(2,1)S(1)} %copy-done.32, bf16[1024,3072]{1,0:T(8,128)(2,1)S(1)} %copy-done.30), kind=kOutput, calls=%fused_computation.1 | convolution fusion | flops 4834197504 | bytes 12582912 | tf_op jit(solution)/shard_map/rd,rf->df/dot_general | solution.py:701
  235.4 1.7 collective-permute-start.3
  237.4 1.8 collective-permute-start.5
  239.2 5.6 %convolution_convert_fusion = bf16[3072,768]{1,0:T(8,128)(2,1)S(1)} fusion(bf16[1024,3072]{1,0:T(8,128)(2,1)S(1)} %bitcast.305, bf16[1024,768]{1,0:T(8,128)(2,1)S(1)} %copy-done.31), kind=kOutput, calls=%fused_computation | convolution fusion | flops 4834197504 | bytes 12582912 | tf_op jit(solution)/shard_map/rf,rd->fd/dot_general | solution.py:700
  249.4 2.5 constant_dynamic-update-slice_fusion
  251.9 3.4 collective-permute-done.5.refs_3_
  259.6 66.7 %att_bwd.1 = (bf16[4096,768]{1,0:T(8,128)(2,1)}, f32[8,768]{1,0:T(8,128)}) custom-call(s32[12288]{0:T(1024)} %bitcast.250, bf16[3,4096,128]{2,1,0:T(8,128)(2,1)} %get-tuple-element.62.left, bf16[3,4096,128]{2,1,0:T(8,128)(2,1)} %get-tuple-element.63.right, bf16[1536,128]{1,0:T(8,128)(2,1)} %get-tuple-element.74.refs_0_, bf16[1536,128]{1,0:T(8,128)(2,1)} %copy-done.5, ...), custom_call_target="tpu_custom_call" | custom-call | tf_op jit(solution)/shard_map/att_bwd/pallas_call | solution.py:180
  327.7 4.5 convolution_convert_fusion.4
  333.3 4.1 convolution_convert_fusion.3
  337.6 2.6 convolution_convert_fusion.2
  340.2 2.2 collective-permute-start.8
  342.5 6.2 %convolution_convert_fusion.5 = bf16[768,768]{1,0:T(8,128)(2,1)} fusion(bf16[4096,768]{1,0:T(8,128)(2,1)S(1)} %bitcast.222, bf16[4096,768]{1,0:T(8,128)(2,1)S(1)} %copy-done.29), kind=kOutput, calls=%fused_computation.13 | convolution fusion | flops 4832428032 | bytes 13762560 | tf_op jit(solution)/shard_map/rd,re->de/dot_general | solution.py:734
  349.7 86.3 %reduce_small.1 = (bf16[2,2,24,768]{3,2,1,0:T(8,128)(2,1)}, f32[8,128]{1,0:T(8,128)}) custom-call(bf16[2,2,2,2,2,24,768]{6,5,4,3,2,1,0:T(8,128)(2,1)} %bitcast.240, f32[2,2,2,2,2,8,128]{6,5,4,3,2,1,0:T(8,128)} %bitcast.248), custom_call_target="tpu_custom_call" | custom-call | tf_op jit(solution)/shard_map/reduce_small/pallas_call | solution.py:576
  440.4 3.0 fusion.3
  443.5 4.9 %add_bitcast_fusion = f32[1,1024,768]{2,1,0:T(8,128)} fusion(bf16[1024,768]{1,0:T(8,128)(2,1)} %collective-permute-done.8, bf16[1024,768]{1,0:T(8,128)(2,1)} %collective-permute-done.7, bf16[1024,768]{1,0:T(8,128)(2,1)} %collective-permute-done.6, f32[1024,768]{1,0:T(8,128)S(1)} %copy-done.2, f32[1024,768]{1,0:T(8,128)S(1)} %fusion.3), kind=kLoop, calls=%fused_computation.2 | loop fusion | flops 5505024 | bytes 14155776 | tf_op jit(solution)/shard_map/broadcast_in_dim | solution.py:774
  448.4 2.2 reduce-scatter.2.cloned.1.call-done
  (210 shorter events, 44.0 us)
Async XLA Ops:
  7.3 4.4 copy-start.16
  7.3 162.8 %all-gather.3.cloned.1.call-start = ((), (), s32[]{:S(2)}) async-start(), calls=%async_computation.2 | async-start | bytes 10948608 | tf_op jit(solution)/shard_map/all_gather | solution.py:596
  80.7 369.8 %reduce-scatter.2.cloned.1.call-start = ((), (), s32[]{:S(2)}) async-start(), calls=%async_computation.1 | async-start | bytes 10948608 | tf_op jit(solution)/shard_map/reduce_scatter | solution.py:600
  162.4 19.2 %collective-permute-start = (bf16[1536,128]{1,0:T(8,128)(2,1)}, bf16[1536,128]{1,0:T(8,128)(2,1)}, u32[]{:S(2)}, u32[]{:S(2)}) collective-permute-start(bf16[1536,128]{1,0:T(8,128)(2,1)} %get-tuple-element.56), channel_id=1, source_target_pairs={{0,4},{4,0},{8,12},{12,8},{16,20},{20,16},{24,28},{28,24},{1,5},{5... | collective-permute-start | bytes 1179656 | tf_op jit(solution)/shard_map/ppermute | solution.py:592
  164.0 17.6 %collective-permute-start.1 = (bf16[1536,128]{1,0:T(8,128)(2,1)}, bf16[1536,128]{1,0:T(8,128)(2,1)}, u32[]{:S(2)}, u32[]{:S(2)}) collective-permute-start(bf16[1536,128]{1,0:T(8,128)(2,1)} %get-tuple-element.57), channel_id=1, source_target_pairs={{0,8},{4,12},{8,0},{12,4},{16,24},{20,28},{24,16},{28,20},{1,9},{5... | collective-permute-start | bytes 1179656 | tf_op jit(solution)/shard_map/ppermute | solution.py:592
  164.8 18.3 %collective-permute-start.2 = (bf16[1536,128]{1,0:T(8,128)(2,1)}, bf16[1536,128]{1,0:T(8,128)(2,1)}, u32[]{:S(2)}, u32[]{:S(2)}) collective-permute-start(bf16[1536,128]{1,0:T(8,128)(2,1)} %get-tuple-element.58), channel_id=1, source_target_pairs={{0,12},{4,8},{8,4},{12,0},{16,28},{20,24},{24,20},{28,16},{1,13},{... | collective-permute-start | bytes 1179656 | tf_op jit(solution)/shard_map/ppermute | solution.py:592
  233.3 5.9 %slice-start.2 = ((s8[6291456]{0:T(1024)(128)(4,1)}), s8[4194304]{0:T(1024)(128)(4,1)S(1)}, s32[]{:S(2)}) async-start(s8[6291456]{0:T(1024)(128)(4,1)} %bitcast.304), calls=%async_computation.5 | async-start | bytes 8388608
  233.6 5.6 %slice-start.3 = ((s8[6291456]{0:T(1024)(128)(4,1)}), s8[2097152]{0:T(1024)(128)(4,1)S(1)}, s32[]{:S(2)}) async-start(s8[6291456]{0:T(1024)(128)(4,1)} %bitcast.304), calls=%async_computation.6 | async-start | bytes 4194304
  234.2 5.0 %copy-start.31 = (bf16[1024,768]{1,0:T(8,128)(2,1)S(1)}, bf16[1024,768]{1,0:T(8,128)(2,1)}, u32[]{:S(2)}) copy-start(bf16[1024,768]{1,0:T(8,128)(2,1)} %get-tuple-element.73) | copy-start | bytes 4718596
  235.4 16.4 %collective-permute-start.3 = (bf16[1536,128]{1,0:T(8,128)(2,1)S(1)}, bf16[1536,128]{1,0:T(8,128)(2,1)S(1)}, u32[]{:S(2)}, u32[]{:S(2)}) collective-permute-start(bf16[1536,128]{1,0:T(8,128)(2,1)S(1)} %copy-done.35), channel_id=1, source_target_pairs={{0,4},{4,0},{8,12},{12,8},{16,20},{20,16},{24,28},{28,24},{1,5},{5... | collective-permute-start | bytes 1179656 | tf_op jit(solution)/shard_map/ppermute | solution.py:592
  237.1 14.7 %collective-permute-start.4 = (bf16[1536,128]{1,0:T(8,128)(2,1)S(1)}, bf16[1536,128]{1,0:T(8,128)(2,1)S(1)}, u32[]{:S(2)}, u32[]{:S(2)}) collective-permute-start(bf16[1536,128]{1,0:T(8,128)(2,1)S(1)} %copy-done.34), channel_id=1, source_target_pairs={{0,8},{4,12},{8,0},{12,4},{16,24},{20,28},{24,16},{28,20},{1,9},{5... | collective-permute-start | bytes 1179656 | tf_op jit(solution)/shard_map/ppermute | solution.py:592
  237.4 17.9 %collective-permute-start.5 = (bf16[1536,128]{1,0:T(8,128)(2,1)S(1)}, bf16[1536,128]{1,0:T(8,128)(2,1)S(1)}, u32[]{:S(2)}, u32[]{:S(2)}) collective-permute-start(bf16[1536,128]{1,0:T(8,128)(2,1)S(1)} %copy-done.33), channel_id=1, source_target_pairs={{0,12},{4,8},{8,4},{12,0},{16,28},{20,24},{24,20},{28,16},{1,13},{... | collective-permute-start | bytes 1179656 | tf_op jit(solution)/shard_map/ppermute | solution.py:592
  327.7 5.7 %copy-start = (bf16[1,32,24,768]{3,2,1,0:T(8,128)(2,1)S(1)}, bf16[1,32,24,768]{3,2,1,0:T(8,128)(2,1)}, u32[]{:S(2)}) copy-start(bf16[1,32,24,768]{3,2,1,0:T(8,128)(2,1)} %constant_dynamic-slice_fusion.2) | copy-start | bytes 3538948
  327.7 10.0 %copy-start.29 = (bf16[4096,768]{1,0:T(8,128)(2,1)S(1)}, bf16[4096,768]{1,0:T(8,128)(2,1)}, u32[]{:S(2)}) copy-start(bf16[4096,768]{1,0:T(8,128)(2,1)} %get-tuple-element.78) | copy-start | bytes 18874372
  327.7 14.7 %slice-start = ((s8[6291456]{0:T(1024)(128)(4,1)}), s8[4194304]{0:T(1024)(128)(4,1)S(1)}, s32[]{:S(2)}) async-start(s8[6291456]{0:T(1024)(128)(4,1)} %bitcast.220), calls=%async_computation.3 | async-start | bytes 8388608
  332.2 10.2 %slice-start.1 = ((s8[6291456]{0:T(1024)(128)(4,1)}), s8[2097152]{0:T(1024)(128)(4,1)S(1)}, s32[]{:S(2)}) async-start(s8[6291456]{0:T(1024)(128)(4,1)} %bitcast.220), calls=%async_computation.4 | async-start | bytes 4194304
  332.2 111.2 %collective-permute-start.6 = (bf16[1024,768]{1,0:T(8,128)(2,1)}, bf16[1024,768]{1,0:T(8,128)(2,1)}, u32[]{:S(2)}, u32[]{:S(2)}) collective-permute-start(bf16[1024,768]{1,0:T(8,128)(2,1)} %convolution_convert_fusion.4), channel_id=1, source_target_pairs={{0,4},{4,0},{8,12},{12,8},{16,20},{20,16},{24,28},{28,24},{1,5},{5... | collective-permute-start | bytes 4718600 | tf_op jit(solution)/shard_map/ppermute | solution.py:592
  337.4 106.0 %collective-permute-start.7 = (bf16[1024,768]{1,0:T(8,128)(2,1)}, bf16[1024,768]{1,0:T(8,128)(2,1)}, u32[]{:S(2)}, u32[]{:S(2)}) collective-permute-start(bf16[1024,768]{1,0:T(8,128)(2,1)} %convolution_convert_fusion.3), channel_id=1, source_target_pairs={{0,8},{4,12},{8,0},{12,4},{16,24},{20,28},{24,16},{28,20},{1,9},{5... | collective-permute-start | bytes 4718600 | tf_op jit(solution)/shard_map/ppermute | solution.py:592
  340.2 103.2 %collective-permute-start.8 = (bf16[1024,768]{1,0:T(8,128)(2,1)}, bf16[1024,768]{1,0:T(8,128)(2,1)}, u32[]{:S(2)}, u32[]{:S(2)}) collective-permute-start(bf16[1024,768]{1,0:T(8,128)(2,1)} %convolution_convert_fusion.2), channel_id=1, source_target_pairs={{0,12},{4,8},{8,4},{12,0},{16,28},{20,24},{24,20},{28,16},{1,13},{... | collective-permute-start | bytes 4718600 | tf_op jit(solution)/shard_map/ppermute | solution.py:592
  342.4 6.2 %copy-start.13 = (f32[1,32,24]{2,1,0:T(8,128)S(1)}, f32[1,32,24]{2,1,0:T(8,128)}, u32[]{:S(2)}) copy-start(f32[1,32,24]{2,1,0:T(8,128)} %concatenate.76) | copy-start | bytes 9220
  342.4 6.2 %copy-start.11 = (f32[2,32,24]{2,1,0:T(8,128)S(1)}, f32[2,32,24]{2,1,0:T(8,128)}, u32[]{:S(2)}) copy-start(f32[2,32,24]{2,1,0:T(8,128)} %concatenate.77) | copy-start | bytes 18436
  342.5 6.2 %copy-start.14 = (f32[1,32,24]{2,1,0:T(8,128)S(1)}, f32[1,32,24]{2,1,0:T(8,128)}, u32[]{:S(2)}) copy-start(f32[1,32,24]{2,1,0:T(8,128)} %concatenate.78) | copy-start | bytes 9220
  342.5 6.2 %copy-start.12 = (f32[2,32,24]{2,1,0:T(8,128)S(1)}, f32[2,32,24]{2,1,0:T(8,128)}, u32[]{:S(2)}) copy-start(f32[2,32,24]{2,1,0:T(8,128)} %concatenate.79) | copy-start | bytes 18436
  342.5 6.4 %copy-start.15 = (f32[32,96]{1,0:T(8,128)S(1)}, f32[32,96]{1,0:T(8,128)}, u32[]{:S(2)}) copy-start(f32[32,96]{1,0:T(8,128)} %reshape.177) | copy-start | bytes 36868
  (27 other events, 78.7 us)
Sparse Core Ops, SparseCore 0:
  80.8 86.4 all-gather.2
  255.5 195.0 reduce-scatter.1
where the time goes:
time: 461 us
  Pallas kernels  334 us (72%)
  local copies, waits for them, and re-layouts  46.6 us (10%)
  matrix products  34.8 us (8%)
  between operations  15 us (3%)
  other arithmetic  11.8 us (3%)
  starting transfers between devices  10.8 us (2%)
  waiting for transfers between devices  7.16 us (2%)
    pallas_call x1, Pallas kernels, reduce_small(): pl.pallas_call(functools.partial(reduce_kernel, nt, ng), out_shape=[S((2,...  86.3 us
    pallas_call x1, Pallas kernels, fwd(): pl.pallas_call(functools.partial(fwd_kernel, span), grid=(H,), out_shape=...  74.3 us
    pallas_call x1, Pallas kernels, collect(): pl.pallas_call(functools.partial(collect_kernel, nt, ng, parts), out_shap...  67.1 us
    pallas_call x1, Pallas kernels, bwd(): pl.pallas_call(functools.partial(bwd_kernel, span), grid=(H,), out_shape=...  66.7 us
    pallas_call x1, Pallas kernels, mid(): pl.pallas_call(functools.partial(mid_kernel, span), grid=(count // rows,)...  39.9 us
    dot_general x4, matrix products, shards(): jnp.einsum('re,de->rd', grad_rows[k * count:(k + 1) * count], arranged, p...  14.2 us
    unnamed x110, local copies, waits for them, and re-layouts  11.6 us
    ppermute x9, starting transfers between devices, flip(): return lax.ppermute(block, 'tok', [(i, i ^ mask) for i in range(count)])  10.8 us
  transfers between devices with their start and end apart: 11, of which 3 were waited for; matrix products, arithmetic and copies ran while one was open for 15% of the time, Pallas kernels for 49%

commit v1 on v0

--- a/solution.py
+++ b/solution.py
@@ -56,18 +56,18 @@
             ord_[pl.ds(2*pos[h*n+t],2),:]=src[pl.ds(2*t,2),:]
         return 0
     lax.fori_loop(0,n//U,scat,0)
-    CB=4
+    CB=16
     def clus(i,_):
-        for u in range(CB):
-            r=pl.multiple_of((i*CB+u)*CL,CL)
-            l=ord_[pl.ds(2*r,CL,stride=2),:].astype(BF)
-            rr=ord_[pl.ds(2*r+1,CL,stride=2),:].astype(BF)
+        at=[pl.multiple_of((i*CB+u)*CL,CL) for u in range(CB)]
+        ls=[ord_[pl.ds(2*r,CL,stride=2),:].astype(BF) for r in at]
+        rs=[ord_[pl.ds(2*r+1,CL,stride=2),:].astype(BF) for r in at]
+        ss=[nt(rr,l) for rr,l in zip(rs,ls)]
+        for r,l,rr in zip(at,ls,rs):
             left[0,pl.ds(r,CL),:]=l
             right[0,pl.ds(r,CL),:]=rr
-            s=nt(rr,l)
-            m=jnp.max(s,axis=0,keepdims=True)
-            e=jnp.exp((s-m)*0.125)
-            p=(e*(1.0/jnp.sum(e,axis=0,keepdims=True))).astype(BF)
+        es=[jnp.exp((x-jnp.max(x,axis=0,keepdims=True))*0.125) for x in ss]
+        ps=[(e*(1.0/jnp.sum(e,axis=0,keepdims=True))).astype(BF) for e in es]
+        for r,p,rr in zip(at,ps,rs):
             oc[pl.ds(r,CL),:]=tn(p,rr)
         return 0
     lax.fori_loop(0,n//CL//CB,clus,0)
@@ -132,24 +132,20 @@
     lax.fori_loop(0,n//U,scat,0)
     lane=lax.broadcasted_iota(jnp.int32,(CL,128),1)
     mask=(lane<64)==(h==0)
-    CB=4
+    CB=16
     def clus(i,_):
-        for u in range(CB):
-            r=pl.multiple_of((i*CB+u)*CL,CL)
-            l=left[0,pl.ds(r,CL),:]
-            rr=right[0,pl.ds(r,CL),:]
-            d=jnp.where(mask,ord_[pl.ds(r,CL),:],0.0).astype(BF)
-            s=nt(rr,l)
-            m=jnp.max(s,axis=0,keepdims=True)
-            e=jnp.exp((s-m)*0.125)
-            p=e*(1.0/jnp.sum(e,axis=0,keepdims=True))
-            dp=nt(rr,d)
-            rd=jnp.sum(dp*p,axis=0,keepdims=True)
-            ds=(p*(dp-rd)).astype(BF)
-            dl=tn(ds,rr)*0.125
-            dr=nn(ds,l)*0.125+nn(p.astype(BF),d)
-            dc[pl.ds(2*r,CL,stride=2),:]=dl
-            dc[pl.ds(2*r+1,CL,stride=2),:]=dr
+        at=[pl.multiple_of((i*CB+u)*CL,CL) for u in range(CB)]
+        ls=[left[0,pl.ds(r,CL),:] for r in at]
+        rs=[right[0,pl.ds(r,CL),:] for r in at]
+        gs=[jnp.where(mask,ord_[pl.ds(r,CL),:],0.0).astype(BF) for r in at]
+        ss=[nt(rr,l) for rr,l in zip(rs,ls)]
+        dps=[nt(rr,d) for rr,d in zip(rs,gs)]
+        es=[jnp.exp((x-jnp.max(x,axis=0,keepdims=True))*0.125) for x in ss]
+        ps=[e*(1.0/jnp.sum(e,axis=0,keepdims=True)) for e in es]
+        dss=[(p*(dp-jnp.sum(dp*p,axis=0,keepdims=True))).astype(BF) for p,dp in zip(ps,dps)]
+        for r,ds,p,l,rr,d in zip(at,dss,ps,ls,rs,gs):
+            dc[pl.ds(2*r,CL,stride=2),:]=tn(ds,rr)*0.125
+            dc[pl.ds(2*r+1,CL,stride=2),:]=nn(ds,l)*0.125+nn(p.astype(BF),d)
         return 0
     lax.fori_loop(0,n//CL//CB,clus,0)
     def gath(i,_):
@@ -718,7 +714,7 @@
         + [contract_grad.reshape(devices, strips * few, width)],
         axis=1,
     )
-    landed, wide_grad = lax.optimization_barrier((landed, wide_grad))
+    landed, held = lax.optimization_barrier((landed, wide_grad))
     wide_grad = scatter_sum(wide_grad)[0].astype(F32)
     project_out_grad = wide_grad[:few]
     expand_grad = wide_grad[few : (1 + strips) * few].reshape(strips, few, width).transpose(1, 0, 2).reshape(few, -1)

time: 461 us -> 467 us (1.013)
  waiting for transfers between devices: 7.16 us -> 53.6 us
  Pallas kernels: 334 us -> 292 us
    all_gather x1, waiting for transfers between devices: 0.01 us -> 34.3 us  [gather_all(): return lax.all_gather(item, ('tok', 'grp'), axis=0, tiled=True)]
    pallas_call x1, Pallas kernels: 74.3 us -> 50.3 us  [fwd(): pl.pallas_call(functools.partial(fwd_kernel, span), grid=(H,), out_shape=...]
    pallas_call x1, Pallas kernels: 66.7 us -> 45.5 us  [bwd(): pl.pallas_call(functools.partial(bwd_kernel, span), grid=(H,), out_shape=...]
    ppermute x9, waiting for transfers between devices: 4.96 us -> 14 us  [flip(): return lax.ppermute(block, 'tok', [(i, i ^ mask) for i in range(count)])]
    unnamed x110 -> x104, local copies, waits for them, and re-layouts: 11.6 us -> 13.6 us
  transfers between devices with their start and end apart: 11 -> 11, of which waited for: 3 -> 5; matrix products, arithmetic and copies ran while one was open for 15% -> 12% of each run, Pallas kernels for 49% -> 40%
where the time goes in v1:
time: 467 us
  Pallas kernels  292 us (63%)
  waiting for transfers between devices  53.6 us (11%)
  local copies, waits for them, and re-layouts  48.7 us (10%)
  matrix products  34.6 us (7%)
  between operations  14.9 us (3%)
  other arithmetic  11.8 us (3%)
  starting transfers between devices  10.9 us (2%)
    pallas_call x1, Pallas kernels, reduce_small(): pl.pallas_call(functools.partial(reduce_kernel, nt, ng), out_shape=[S((2,...  89.1 us
    pallas_call x1, Pallas kernels, collect(): pl.pallas_call(functools.partial(collect_kernel, nt, ng, parts), out_shap...  67.2 us
    pallas_call x1, Pallas kernels, fwd(): pl.pallas_call(functools.partial(fwd_kernel, span), grid=(H,), out_shape=...  50.3 us
    pallas_call x1, Pallas kernels, bwd(): pl.pallas_call(functools.partial(bwd_kernel, span), grid=(H,), out_shape=...  45.5 us
    pallas_call x1, Pallas kernels, mid(): pl.pallas_call(functools.partial(mid_kernel, span), grid=(count // rows,)...  40.1 us
    all_gather x1, waiting for transfers between devices, gather_all(): return lax.all_gather(item, ('tok', 'grp'), axis=0, tiled=True)  34.3 us
    dot_general x4, matrix products, shards(): jnp.einsum('re,de->rd', grad_rows[k * count:(k + 1) * count], arranged, p...  14 us
    ppermute x9, waiting for transfers between devices, flip(): return lax.ppermute(block, 'tok', [(i, i ^ mask) for i in range(count)])  14 us
  transfers between devices with their start and end apart: 11, of which 5 were waited for; matrix products, arithmetic and copies ran while one was open for 12% of the time, Pallas kernels for 40%

profile of v1, /device:TPU:0, one launch (start us, length us, event | category | flops | bytes accessed | tf_op | source)
XLA Modules:
  0.0 466.7 jit_solution(3813058826691457307)
XLA Ops:
  13.6 67.2 %collect.1 = (bf16[4,1024,768]{2,1,0:T(8,128)(2,1)}, s32[4,3,1024]{2,1,0:T(4,128)}, bf16[2,2,2,2,2,2,2,24,768]{8,7,6,5,4,3,2,1,0:T(8,128)(2,1)}, f32[2,2,2,2,2,8,128]{6,5,4,3,2,1,0:T(8,128)}) custom-call(bf16[1024,768]{1,0:T(8,128)(2,1)} %bitcast.223, s32[4,3,1024]{2,1,0:T(4,128)} %add_select_fusion.refs_1_, bf16[2,2,24,768]{3,2,1,0:T(8,128)(2,1)} %bitcast.245, ...), custom_call_target="tpu_custom_call" | custom-call | tf_op jit(solution)/shard_map/collect/pallas_call | solution.py:463
  85.8 2.4 constant_dynamic-slice_fusion.2
  88.2 50.3 %att_fwd.1 = (bf16[1536,128]{1,0:T(8,128)(2,1)}, bf16[1536,128]{1,0:T(8,128)(2,1)}, bf16[1536,128]{1,0:T(8,128)(2,1)}, bf16[1536,128]{1,0:T(8,128)(2,1)}, bf16[3...) custom-call(s32[12288]{0:T(1024)} %bitcast.249, bf16[4096,768]{1,0:T(8,128)(2,1)} %bitcast.219, ...), custom_call_target="tpu_custom_call" | custom-call | tf_op jit(solution)/shard_map/att_fwd/pallas_call | solution.py:99
  146.2 34.3 %all-gather.3.cloned.1.call-done = bf16[6912,768]{1,0:T(8,128)(2,1)} async-done(((bf16[216,768]{1,0:T(8,128)(2,1)}), bf16[6912,768]{1,0:T(8,128)(2,1)}) %all-gather.3.cloned.1.call-update) | async-done | bytes 10616848 | tf_op jit(solution)/shard_map/all_gather | solution.py:592
  180.5 2.4 slice.534
  182.9 6.5 %fusion.9 = (bf16[32,96,768]{2,1,0:T(8,128)(2,1)}, bf16[32,96,768]{2,1,0:T(8,128)(2,1)S(1)}) fusion(bf16[32,216,768]{2,1,0:T(8,128)(2,1)} %bitcast.218), kind=kLoop, calls=%fused_computation.106 | loop fusion | bytes 18874368 | tf_op jit(solution)/shard_map/slice | solution.py:661
  189.4 2.5 copy.2015
  191.9 40.1 %mid.1 = (bf16[1024,768]{1,0:T(8,128)(2,1)}, f32[1024,768]{1,0:T(8,128)}, bf16[1536,128]{1,0:T(8,128)(2,1)}, bf16[1536,128]{1,0:T(8,128)(2,1)}, bf16[1536,128]{1...) custom-call(bf16[1536,128]{1,0:T(8,128)(2,1)} %get-tuple-element.54., ...), custom_call_target="tpu_custom_call" | custom-call | tf_op jit(solution)/shard_map/mid/pallas_call | solution.py:283
  232.0 3.5 convolution_convert_fusion.6
  237.0 5.4 %convolution_convert_fusion.1 = bf16[768,3072]{1,0:T(8,128)(2,1)S(1)} fusion(bf16[1024,768]{1,0:T(8,128)(2,1)S(1)} %copy-done.29, bf16[1024,3072]{1,0:T(8,128)(2,1)S(1)} %copy-done.27), kind=kOutput, calls=%fused_computation.1 | convolution fusion | flops 4834197504 | bytes 12582912 | tf_op jit(solution)/shard_map/rd,rf->df/dot_general | solution.py:697
  246.3 5.6 %convolution_convert_fusion = bf16[3072,768]{1,0:T(8,128)(2,1)S(1)} fusion(bf16[1024,3072]{1,0:T(8,128)(2,1)S(1)} %bitcast.305, bf16[1024,768]{1,0:T(8,128)(2,1)S(1)} %copy-done.28), kind=kOutput, calls=%fused_computation | convolution fusion | flops 4834197504 | bytes 12582912 | tf_op jit(solution)/shard_map/rf,rd->fd/dot_general | solution.py:696
  256.4 2.6 constant_dynamic-update-slice_fusion
  266.9 4.4 collective-permute-done.3.refs_1_
  271.3 1.9 collective-permute-done.4.refs_2_
  273.2 7.7 %collective-permute-done.5.refs_3_ = bf16[1536,128]{1,0:T(8,128)(2,1)} collective-permute-done((bf16[1536,128]{1,0:T(8,128)(2,1)S(1)}, bf16[1536,128]{1,0:T(8,128)(2,1)}, u32[]{:S(2)}, u32[]{:S(2)}) %collective-permute-start.5) | collective-permute-done | bytes 393248 | tf_op jit(solution)/shard_map/ppermute | solution.py:588
  280.9 45.5 %att_bwd.1 = (bf16[4096,768]{1,0:T(8,128)(2,1)}, f32[8,768]{1,0:T(8,128)}) custom-call(s32[12288]{0:T(1024)} %bitcast.250, bf16[3,4096,128]{2,1,0:T(8,128)(2,1)} %get-tuple-element.61.left, bf16[3,4096,128]{2,1,0:T(8,128)(2,1)} %get-tuple-element.62.right, bf16[1536,128]{1,0:T(8,128)(2,1)} %get-tuple-element.73.refs_0_, ...), custom_call_target="tpu_custom_call" | custom-call | tf_op jit(solution)/shard_map/att_bwd/pallas_call | solution.py:176
  327.8 4.5 convolution_convert_fusion.4
  333.6 4.0 convolution_convert_fusion.3
  339.4 2.6 convolution_convert_fusion.2
  342.8 6.2 %convolution_convert_fusion.5 = bf16[768,768]{1,0:T(8,128)(2,1)} fusion(bf16[4096,768]{1,0:T(8,128)(2,1)S(1)} %bitcast.222, bf16[4096,768]{1,0:T(8,128)(2,1)S(1)} %copy-done.26), kind=kOutput, calls=%fused_computation.13 | convolution fusion | flops 4832428032 | bytes 13762560 | tf_op jit(solution)/shard_map/rd,re->de/dot_general | solution.py:730
  350.0 89.1 %reduce_small.1 = (bf16[2,2,24,768]{3,2,1,0:T(8,128)(2,1)}, f32[8,128]{1,0:T(8,128)}) custom-call(bf16[2,2,2,2,2,24,768]{6,5,4,3,2,1,0:T(8,128)(2,1)} %bitcast.240, f32[2,2,2,2,2,8,128]{6,5,4,3,2,1,0:T(8,128)} %bitcast.248), custom_call_target="tpu_custom_call" | custom-call | tf_op jit(solution)/shard_map/reduce_small/pallas_call | solution.py:572
  443.5 3.0 fusion.3
  446.5 4.9 %add_bitcast_fusion = f32[1,1024,768]{2,1,0:T(8,128)} fusion(bf16[1024,768]{1,0:T(8,128)(2,1)} %collective-permute-done.8, bf16[1024,768]{1,0:T(8,128)(2,1)} %collective-permute-done.7, bf16[1024,768]{1,0:T(8,128)(2,1)} %collective-permute-done.6, f32[1024,768]{1,0:T(8,128)S(1)} %copy-done.2, f32[1024,768]{1,0:T(8,128)S(1)} %fusion.3), kind=kLoop, calls=%fused_computation.2 | loop fusion | flops 5505024 | bytes 14155776 | tf_op jit(solution)/shard_map/broadcast_in_dim | solution.py:770
  451.4 5.2 %reduce-scatter.2.cloned.1.call-done = bf16[1,216,768]{2,1,0:T(8,128)(2,1)} async-done(((bf16[32,216,768]{2,1,0:T(8,128)(2,1)}), bf16[1,216,768]{2,1,0:T(8,128)(2,1)}) %reduce-scatter.2.cloned.1.call-update) | async-done | bytes 331792 | tf_op jit(solution)/shard_map/reduce_scatter | solution.py:596
  (204 shorter events, 50.1 us)
Async XLA Ops:
  7.3 4.4 copy-start.13
  7.3 4.4 copy-start.7
  7.3 173.2 %all-gather.3.cloned.1.call-start = ((), (), s32[]{:S(2)}) async-start(), calls=%async_computation.2 | async-start | bytes 10948608 | tf_op jit(solution)/shard_map/all_gather | solution.py:592
  80.8 375.8 %reduce-scatter.2.cloned.1.call-start = ((), (), s32[]{:S(2)}) async-start(), calls=%async_computation.1 | async-start | bytes 10948608 | tf_op jit(solution)/shard_map/reduce_scatter | solution.py:596
  138.5 53.5 %collective-permute-start = (bf16[1536,128]{1,0:T(8,128)(2,1)}, bf16[1536,128]{1,0:T(8,128)(2,1)}, u32[]{:S(2)}, u32[]{:S(2)}) collective-permute-start(bf16[1536,128]{1,0:T(8,128)(2,1)} %get-tuple-element.55), channel_id=1, source_target_pairs={{0,4},{4,0},{8,12},{12,8},{16,20},{20,16},{24,28},{28,24},{1,5},{5... | collective-permute-start | bytes 1179656 | tf_op jit(solution)/shard_map/ppermute | solution.py:588
  139.9 52.0 %collective-permute-start.1 = (bf16[1536,128]{1,0:T(8,128)(2,1)}, bf16[1536,128]{1,0:T(8,128)(2,1)}, u32[]{:S(2)}, u32[]{:S(2)}) collective-permute-start(bf16[1536,128]{1,0:T(8,128)(2,1)} %get-tuple-element.56), channel_id=1, source_target_pairs={{0,8},{4,12},{8,0},{12,4},{16,24},{20,28},{24,16},{28,20},{1,9},{5... | collective-permute-start | bytes 1179656 | tf_op jit(solution)/shard_map/ppermute | solution.py:588
  140.8 51.1 %collective-permute-start.2 = (bf16[1536,128]{1,0:T(8,128)(2,1)}, bf16[1536,128]{1,0:T(8,128)(2,1)}, u32[]{:S(2)}, u32[]{:S(2)}) collective-permute-start(bf16[1536,128]{1,0:T(8,128)(2,1)} %get-tuple-element.57), channel_id=1, source_target_pairs={{0,12},{4,8},{8,4},{12,0},{16,28},{20,24},{24,20},{28,16},{1,13},{... | collective-permute-start | bytes 1179656 | tf_op jit(solution)/shard_map/ppermute | solution.py:588
  259.0 4.5 copy-start.14
  259.0 7.3 %copy-start.15 = (f32[4,768]{1,0:T(4,128)S(1)}, f32[4,768]{1,0:T(4,128)}, u32[]{:S(2)}) copy-start(f32[4,768]{1,0:T(4,128)} %get-tuple-element.80) | copy-start | bytes 36868
  260.0 11.4 %collective-permute-start.3 = (bf16[1536,128]{1,0:T(8,128)(2,1)S(1)}, bf16[1536,128]{1,0:T(8,128)(2,1)}, u32[]{:S(2)}, u32[]{:S(2)}) collective-permute-start(bf16[1536,128]{1,0:T(8,128)(2,1)S(1)} %copy-done.32), channel_id=1, source_target_pairs={{0,4},{4,0},{8,12},{12,8},{16,20},{20,16},{24,28},{28,24},{1,5},{5... | collective-permute-start | bytes 1179656 | tf_op jit(solution)/shard_map/ppermute | solution.py:588
  261.2 12.1 %collective-permute-start.4 = (bf16[1536,128]{1,0:T(8,128)(2,1)S(1)}, bf16[1536,128]{1,0:T(8,128)(2,1)}, u32[]{:S(2)}, u32[]{:S(2)}) collective-permute-start(bf16[1536,128]{1,0:T(8,128)(2,1)S(1)} %copy-done.31), channel_id=1, source_target_pairs={{0,8},{4,12},{8,0},{12,4},{16,24},{20,28},{24,16},{28,20},{1,9},{5... | collective-permute-start | bytes 1179656 | tf_op jit(solution)/shard_map/ppermute | solution.py:588
  263.0 18.0 %collective-permute-start.5 = (bf16[1536,128]{1,0:T(8,128)(2,1)S(1)}, bf16[1536,128]{1,0:T(8,128)(2,1)}, u32[]{:S(2)}, u32[]{:S(2)}) collective-permute-start(bf16[1536,128]{1,0:T(8,128)(2,1)S(1)} %copy-done.30), channel_id=1, source_target_pairs={{0,12},{4,8},{8,4},{12,0},{16,28},{20,24},{24,20},{28,16},{1,13},{... | collective-permute-start | bytes 1179656 | tf_op jit(solution)/shard_map/ppermute | solution.py:588
  327.8 5.8 %copy-start = (bf16[1,32,24,768]{3,2,1,0:T(8,128)(2,1)S(1)}, bf16[1,32,24,768]{3,2,1,0:T(8,128)(2,1)}, u32[]{:S(2)}) copy-start(bf16[1,32,24,768]{3,2,1,0:T(8,128)(2,1)} %constant_dynamic-slice_fusion.2) | copy-start | bytes 3538948
  327.8 11.6 %copy-start.26 = (bf16[4096,768]{1,0:T(8,128)(2,1)S(1)}, bf16[4096,768]{1,0:T(8,128)(2,1)}, u32[]{:S(2)}) copy-start(bf16[4096,768]{1,0:T(8,128)(2,1)} %get-tuple-element.77) | copy-start | bytes 18874372
  327.8 14.9 %slice-start = ((s8[6291456]{0:T(1024)(128)(4,1)}), s8[4194304]{0:T(1024)(128)(4,1)S(1)}, s32[]{:S(2)}) async-start(s8[6291456]{0:T(1024)(128)(4,1)} %bitcast.220), calls=%async_computation.3 | async-start | bytes 8388608
  332.3 10.4 %slice-start.1 = ((s8[6291456]{0:T(1024)(128)(4,1)}), s8[2097152]{0:T(1024)(128)(4,1)S(1)}, s32[]{:S(2)}) async-start(s8[6291456]{0:T(1024)(128)(4,1)} %bitcast.220), calls=%async_computation.4 | async-start | bytes 4194304
  332.3 114.1 %collective-permute-start.6 = (bf16[1024,768]{1,0:T(8,128)(2,1)}, bf16[1024,768]{1,0:T(8,128)(2,1)}, u32[]{:S(2)}, u32[]{:S(2)}) collective-permute-start(bf16[1024,768]{1,0:T(8,128)(2,1)} %convolution_convert_fusion.4), channel_id=1, source_target_pairs={{0,4},{4,0},{8,12},{12,8},{16,20},{20,16},{24,28},{28,24},{1,5},{5... | collective-permute-start | bytes 4718600 | tf_op jit(solution)/shard_map/ppermute | solution.py:588
  337.6 108.9 %collective-permute-start.7 = (bf16[1024,768]{1,0:T(8,128)(2,1)}, bf16[1024,768]{1,0:T(8,128)(2,1)}, u32[]{:S(2)}, u32[]{:S(2)}) collective-permute-start(bf16[1024,768]{1,0:T(8,128)(2,1)} %convolution_convert_fusion.3), channel_id=1, source_target_pairs={{0,8},{4,12},{8,0},{12,4},{16,24},{20,28},{24,16},{28,20},{1,9},{5... | collective-permute-start | bytes 4718600 | tf_op jit(solution)/shard_map/ppermute | solution.py:588
  342.0 104.5 %collective-permute-start.8 = (bf16[1024,768]{1,0:T(8,128)(2,1)}, bf16[1024,768]{1,0:T(8,128)(2,1)}, u32[]{:S(2)}, u32[]{:S(2)}) collective-permute-start(bf16[1024,768]{1,0:T(8,128)(2,1)} %convolution_convert_fusion.2), channel_id=1, source_target_pairs={{0,12},{4,8},{8,4},{12,0},{16,28},{20,24},{24,20},{28,16},{1,13},{... | collective-permute-start | bytes 4718600 | tf_op jit(solution)/shard_map/ppermute | solution.py:588
  342.8 6.2 %copy-start.10 = (f32[1,32,24]{2,1,0:T(8,128)S(1)}, f32[1,32,24]{2,1,0:T(8,128)}, u32[]{:S(2)}) copy-start(f32[1,32,24]{2,1,0:T(8,128)} %concatenate.76) | copy-start | bytes 9220
  342.8 6.2 %copy-start.8 = (f32[2,32,24]{2,1,0:T(8,128)S(1)}, f32[2,32,24]{2,1,0:T(8,128)}, u32[]{:S(2)}) copy-start(f32[2,32,24]{2,1,0:T(8,128)} %concatenate.77) | copy-start | bytes 18436
  342.8 6.2 %copy-start.11 = (f32[1,32,24]{2,1,0:T(8,128)S(1)}, f32[1,32,24]{2,1,0:T(8,128)}, u32[]{:S(2)}) copy-start(f32[1,32,24]{2,1,0:T(8,128)} %concatenate.78) | copy-start | bytes 9220
  342.8 6.2 %copy-start.9 = (f32[2,32,24]{2,1,0:T(8,128)S(1)}, f32[2,32,24]{2,1,0:T(8,128)}, u32[]{:S(2)}) copy-start(f32[2,32,24]{2,1,0:T(8,128)} %concatenate.79) | copy-start | bytes 18436
  342.8 6.4 %copy-start.12 = (f32[32,96]{1,0:T(8,128)S(1)}, f32[32,96]{1,0:T(8,128)}, u32[]{:S(2)}) copy-start(f32[32,96]{1,0:T(8,128)} %reshape.177) | copy-start | bytes 36868
  (24 other events, 70.5 us)
Sparse Core Ops, SparseCore 0:
  80.9 99.5 all-gather.2
  259.1 197.4 reduce-scatter.1
